TPU v7x, 512 devices: a whole 4x8x8 slice. The times are simulated.
512 devices in a mesh: cache: 64 (over x, z, core), rank: 8 (over y).
Axes of the slice: x: 4, y: 8, z: 8, core: 2. Of those that a mesh axis runs over, the one named last changes fastest.
Arguments:
- cand_rows: bfloat16 [64, 64, 4, 1024], P('cache', None, None, 'rank'), may hold values from -48 to 48
- listed: int32 [64], replicated, may hold values from 0 to 63, each once
- hist_len: int32 [64], P('cache'), may hold values from 768 to 3072, as said below
- block_mask: int32 [64, 24], P('cache'), may hold values 0 or 1
- hist_keys: bfloat16 [1, 64, 3072, 1024], P(None, 'cache', None, 'rank'), may hold values from -6 to 6
- hist_values: bfloat16 [1, 64, 3072, 1024], P(None, 'cache', None, 'rank'), may hold values from -6 to 6
- w_query: bfloat16 [1, 1024, 1024], P(None, None, 'rank'), may hold values from -0.1875 to 0.1875
- w_gate: bfloat16 [1, 1024, 1024], P(None, None, 'rank'), may hold values from -0.1875 to 0.1875
- w_out: bfloat16 [1, 1024, 1024], P(None, None, 'rank'), may hold values from -0.1875 to 0.1875
Outputs:
- ranked: bfloat16 [64, 64, 4, 1024], P('cache', None, None, 'rank')
Inputs may be any that keep to these rules, and one draw needn't show every extreme that they name: `hist_len`: some user has exactly 3072 history events. `listed`: each user id appears once.
All inputs are finite; a program needn't handle non-finite values. No bound on the sum of `block_mask` on one device may be relied on, other than what follows from the above.
Results may differ from a plain program's by a relative error of at most 0.0024.
Values may be sent and summed in bfloat16 or wider, within the bound.
A program may use at most 64 MiB of HBM per device.

v0:
```python
import jax
import jax.numpy as jnp
from jax import lax
from jax.sharding import PartitionSpec as P

D = 1024
HEADS = 8
BLOCK = 128
EPSILON = 1e-05
GROUP_BLOCKS = 4


def head_norm(values):
    centre = jnp.mean(values, axis=-1, keepdims=True)
    spread = jnp.mean(jnp.square(values - centre), axis=-1, keepdims=True)
    return (values - centre) * lax.rsqrt(spread + EPSILON)


def attend(queries, key_cache, value_cache, length, block_list, block_live, turn_count):
    head_size = queries.shape[-1]
    score_scale = head_size ** (-0.5)
    within = jnp.arange(BLOCK, dtype=jnp.int32)
    running = jnp.zeros(queries.shape, jnp.float32)

    def one_turn(turn_no, running):
        chosen = lax.dynamic_slice_in_dim(block_list, turn_no * GROUP_BLOCKS, GROUP_BLOCKS)
        chosen_live = lax.dynamic_slice_in_dim(block_live, turn_no * GROUP_BLOCKS, GROUP_BLOCKS)
        key_rows = jnp.take(key_cache, chosen, axis=0).reshape(
            GROUP_BLOCKS * BLOCK, key_cache.shape[2], head_size
        )
        value_rows = jnp.take(value_cache, chosen, axis=0).reshape(
            GROUP_BLOCKS * BLOCK, key_cache.shape[2], head_size
        )
        places = (chosen[:, None] * BLOCK + within[None, :]).reshape(GROUP_BLOCKS * BLOCK)
        live_mask = ((places < length) & jnp.repeat(chosen_live, BLOCK)).astype(jnp.float32)
        scores = (
            jnp.einsum("nkhe,the->nkht", queries, key_rows, preferred_element_type=jnp.float32)
            * score_scale
        )
        weights = (jax.nn.silu(scores) * live_mask).astype(jnp.bfloat16)
        return running + jnp.einsum(
            "nkht,the->nkhe", weights, value_rows, preferred_element_type=jnp.float32
        )

    return lax.fori_loop(0, turn_count, one_turn, running)


def finish(result):
    return lax.all_to_all(result, "cache", split_axis=0, concat_axis=1, tiled=True)


def on_device(
    cand_rows, listed, hist_len, block_mask, hist_keys, hist_values, w_query, w_gate, w_out
):
    head_size = D // HEADS
    local_width = w_query.shape[2]
    local_heads = local_width // head_size
    blocks_total = block_mask.shape[1]
    padded = -(-blocks_total // GROUP_BLOCKS) * GROUP_BLOCKS
    slot_of_user = jnp.argsort(listed)
    outgoing = jnp.take(cand_rows, slot_of_user, axis=1)
    length = hist_len[0]
    starts = jnp.arange(blocks_total, dtype=jnp.int32) * BLOCK
    usable = (block_mask[0] == 1) & (starts < length)
    filler = jnp.zeros((padded - blocks_total,), jnp.int32)
    block_list = jnp.concatenate([jnp.arange(blocks_total, dtype=jnp.int32), filler])
    block_live = jnp.concatenate([usable, filler > 0])
    turn_count = padded // GROUP_BLOCKS
    current = lax.all_to_all(outgoing, "cache", split_axis=1, concat_axis=0, tiled=True)
    whole_rows = lax.all_gather(current, "rank", axis=3, tiled=True)
    normed = head_norm(whole_rows.astype(jnp.float32)).astype(jnp.bfloat16)
    queries = jax.nn.silu(
        jnp.einsum("nukd,de->nuke", normed, w_query[0], preferred_element_type=jnp.float32)
    ).astype(jnp.bfloat16)
    gate_act = jax.nn.silu(
        jnp.einsum("nukd,de->nuke", normed, w_gate[0], preferred_element_type=jnp.float32)
    )
    split_shape = queries.shape[:3] + (local_heads, head_size)
    queries = queries.reshape(split_shape)
    length, block_list, block_live, turn_count = (length, block_list, block_live, turn_count)
    key_cache = hist_keys[0, 0].reshape(blocks_total, BLOCK, local_heads, head_size)
    value_cache = hist_values[0, 0].reshape(blocks_total, BLOCK, local_heads, head_size)
    attended_list = [
        attend(queries[:, 0], key_cache, value_cache, length, block_list, block_live, turn_count)
    ]
    attended = jnp.stack(attended_list, axis=1)
    hidden = (
        (head_norm(attended) * gate_act.reshape(split_shape))
        .reshape(queries.shape[:3] + (local_width,))
        .astype(jnp.bfloat16)
    )
    rows_in = w_out[0]
    projected = jnp.einsum(
        "nukd,de->nuke",
        lax.all_gather(hidden, "rank", axis=3, tiled=True),
        rows_in,
        preferred_element_type=jnp.float32,
    )
    current = (current.astype(jnp.float32) + projected).astype(jnp.bfloat16)
    returned = finish(current)
    return jnp.take(returned, listed, axis=1)


def solution(mesh):
    placed = (
        P("cache", None, None, "rank"),
        P(),
        P("cache"),
        P("cache", None),
        P(None, "cache", None, "rank"),
        P(None, "cache", None, "rank"),
        P(None, None, "rank"),
        P(None, None, "rank"),
        P(None, None, "rank"),
    )
    return jax.shard_map(
        on_device,
        mesh=mesh,
        in_specs=placed,
        out_specs=P("cache", None, None, "rank"),
        check_vma=False,
    )
```

profile of v0, /device:TPU:1, one launch (start us, length us, event | category | flops | bytes accessed | tf_op | source)
XLA Modules:
  0.0 122.2 jit_solution(12769290152046905703)
XLA Ops:
  0.0 0.7 copy-done.4
  0.7 2.0 %sort.17 = (s32[64]{0:T(128)}, s32[64]{0:T(128)S(1)}) sort(s32[64]{0:T(128)S(1)} %copy-done.4, s32[64]{0:T(128)S(1)} %iota.13), dimensions={0}, to_apply=%region_0.0 | sort | flops 384 | bytes 1024 | tf_op jit(solution)/shard_map/jit(argsort)/sort | solution.py:60
  2.8 1.5 %gather_fusion.2 = bf16[64,4,128]{2,1,0:T(4,128)(2,1)S(1)} fusion(bf16[64,4,128]{2,1,0:T(4,128)(2,1)} %bitcast.138, s32[1024]{0:T(1024)S(1)} %pad_clamp_fusion.2), kind=kCustom, calls=%fused_computation.clone | custom fusion | bytes 131328 | tf_op jit(solution)/shard_map/jit(_take)/gather | solution.py:61
  4.3 0.8 fusion.45
  5.0 14.8 %all-to-all-start = ((bf16[1,64,4,128]{3,2,0,1:T(4,128)(2,1)}), bf16[1,64,4,128]{3,2,0,1:T(4,128)(2,1)S(1)}, u32[]{:S(2)}, u32[]{:S(2)}) async-start(bf16[1,64,4,128]{3,2,0,1:T(4,128)(2,1)} %fusion.45), calls=%async_computation | async-start | bytes 131072 | tf_op jit(solution)/shard_map/all_to_all | solution.py:69
  20.6 0.6 copy-done.3
  21.2 8.5 %all-to-all-done = bf16[1,64,4,128]{3,2,0,1:T(4,128)(2,1)S(1)} async-done(((bf16[1,64,4,128]{3,2,0,1:T(4,128)(2,1)}), bf16[1,64,4,128]{3,2,0,1:T(4,128)(2,1)S(1)}, u32[]{:S(2)}, u32[]{:S(2)}) %all-to-all-start) | async-done | bytes 65568 | tf_op jit(solution)/shard_map/all_to_all | solution.py:69
  29.7 15.8 %all-gather = bf16[1,64,4,1024]{3,2,0,1:T(4,128)(2,1)S(1)} all-gather(bf16[1,64,4,128]{3,2,0,1:T(4,128)(2,1)S(1)} %all-to-all-done), channel_id=2, replica_groups=mesh['cache'=64,'rank'=8] {'rank'}, dimensions={3}, use_global_device_ids=true | all-gather | bytes 589824 | tf_op jit(solution)/shard_map/all_gather | solution.py:70
  45.5 0.3 convert_reduce_fusion
  45.8 0.5 fusion.19
  46.3 0.3 fusion.21
  46.6 0.3 fusion.40
  47.0 29.7 %while.14 = (s32[]{:T(128)}, f32[64,4,1,128]{3,0,1,2:T(8,128)S(1)}, s32[24]{0:T(128)S(1)}, bf16[24,128,1,128]{3,1,0,2:T(8,128)(2,1)}, bf16[24,128,1,128]{3,1,0,2...) while((s32[]{:T(128)}, f32[64,4,1,128]{3,0,1,2:T(8,128)S(1)}, ...), condition=%wide.region_4.7_spmd.clone, body=%wide.region_3.6_spmd.clone.sunk | while | flops 68226080 | bytes 1646929 | solution.py:45
  47.0 0.1 compare_and_fusion.4
  47.1 1.7 %gather_fusion = bf16[4,128,128]{2,1,0:T(8,128)(2,1)S(1)} fusion(bf16[24,128,128]{2,1,0:T(8,128)(2,1)} %bitcast.136, s32[1024]{0:T(1024)S(1)} %pad_clamp_fusion.4), kind=kCustom, calls=%fused_computation.3.clone.clone.1 | custom fusion | bytes 262160 | tf_op jit(solution)/shard_map/while/body/eval_jaxpr/jit(_take)/gather | solution.py:28
  48.8 1.7 %gather_fusion.1 = bf16[4,128,128]{2,1,0:T(8,128)(2,1)S(1)} fusion(bf16[24,128,128]{2,1,0:T(8,128)(2,1)} %bitcast.134, s32[1024]{0:T(1024)S(1)} %pad_clamp_fusion.4), kind=kCustom, calls=%fused_computation.1.clone.clone.1 | custom fusion | bytes 262160 | tf_op jit(solution)/shard_map/while/body/eval_jaxpr/jit(_take)/gather | solution.py:31
  50.5 0.1 bitcast_select_fusion.5
  50.6 0.1 broadcast_multiply_fusion.4
  50.8 0.7 convert_bitcast_fusion.3
  51.5 0.4 fusion.56
  51.9 0.1 compare_and_fusion.4
  52.0 1.7 %gather_fusion = bf16[4,128,128]{2,1,0:T(8,128)(2,1)S(1)} fusion(bf16[24,128,128]{2,1,0:T(8,128)(2,1)} %bitcast.136, s32[1024]{0:T(1024)S(1)} %pad_clamp_fusion.4), kind=kCustom, calls=%fused_computation.3.clone.clone.1 | custom fusion | bytes 262160 | tf_op jit(solution)/shard_map/while/body/eval_jaxpr/jit(_take)/gather | solution.py:28
  53.7 1.7 %gather_fusion.1 = bf16[4,128,128]{2,1,0:T(8,128)(2,1)S(1)} fusion(bf16[24,128,128]{2,1,0:T(8,128)(2,1)} %bitcast.134, s32[1024]{0:T(1024)S(1)} %pad_clamp_fusion.4), kind=kCustom, calls=%fused_computation.1.clone.clone.1 | custom fusion | bytes 262160 | tf_op jit(solution)/shard_map/while/body/eval_jaxpr/jit(_take)/gather | solution.py:31
  55.5 0.1 bitcast_select_fusion.5
  55.5 0.1 broadcast_multiply_fusion.4
  55.7 0.7 convert_bitcast_fusion.3
  56.4 0.4 fusion.56
  56.9 0.1 compare_and_fusion.4
  57.0 1.7 %gather_fusion = bf16[4,128,128]{2,1,0:T(8,128)(2,1)S(1)} fusion(bf16[24,128,128]{2,1,0:T(8,128)(2,1)} %bitcast.136, s32[1024]{0:T(1024)S(1)} %pad_clamp_fusion.4), kind=kCustom, calls=%fused_computation.3.clone.clone.1 | custom fusion | bytes 262160 | tf_op jit(solution)/shard_map/while/body/eval_jaxpr/jit(_take)/gather | solution.py:28
  58.7 1.7 %gather_fusion.1 = bf16[4,128,128]{2,1,0:T(8,128)(2,1)S(1)} fusion(bf16[24,128,128]{2,1,0:T(8,128)(2,1)} %bitcast.134, s32[1024]{0:T(1024)S(1)} %pad_clamp_fusion.4), kind=kCustom, calls=%fused_computation.1.clone.clone.1 | custom fusion | bytes 262160 | tf_op jit(solution)/shard_map/while/body/eval_jaxpr/jit(_take)/gather | solution.py:31
  60.4 0.1 bitcast_select_fusion.5
  60.5 0.1 broadcast_multiply_fusion.4
  60.7 0.7 convert_bitcast_fusion.3
  61.4 0.4 fusion.56
  61.8 0.1 compare_and_fusion.4
  61.9 1.7 %gather_fusion = bf16[4,128,128]{2,1,0:T(8,128)(2,1)S(1)} fusion(bf16[24,128,128]{2,1,0:T(8,128)(2,1)} %bitcast.136, s32[1024]{0:T(1024)S(1)} %pad_clamp_fusion.4), kind=kCustom, calls=%fused_computation.3.clone.clone.1 | custom fusion | bytes 262160 | tf_op jit(solution)/shard_map/while/body/eval_jaxpr/jit(_take)/gather | solution.py:28
  63.6 1.7 %gather_fusion.1 = bf16[4,128,128]{2,1,0:T(8,128)(2,1)S(1)} fusion(bf16[24,128,128]{2,1,0:T(8,128)(2,1)} %bitcast.134, s32[1024]{0:T(1024)S(1)} %pad_clamp_fusion.4), kind=kCustom, calls=%fused_computation.1.clone.clone.1 | custom fusion | bytes 262160 | tf_op jit(solution)/shard_map/while/body/eval_jaxpr/jit(_take)/gather | solution.py:31
  65.4 0.1 bitcast_select_fusion.5
  65.5 0.1 broadcast_multiply_fusion.4
  65.6 0.7 convert_bitcast_fusion.3
  66.3 0.4 fusion.56
  66.8 0.1 compare_and_fusion.4
  66.9 1.7 %gather_fusion = bf16[4,128,128]{2,1,0:T(8,128)(2,1)S(1)} fusion(bf16[24,128,128]{2,1,0:T(8,128)(2,1)} %bitcast.136, s32[1024]{0:T(1024)S(1)} %pad_clamp_fusion.4), kind=kCustom, calls=%fused_computation.3.clone.clone.1 | custom fusion | bytes 262160 | tf_op jit(solution)/shard_map/while/body/eval_jaxpr/jit(_take)/gather | solution.py:28
  68.6 1.7 %gather_fusion.1 = bf16[4,128,128]{2,1,0:T(8,128)(2,1)S(1)} fusion(bf16[24,128,128]{2,1,0:T(8,128)(2,1)} %bitcast.134, s32[1024]{0:T(1024)S(1)} %pad_clamp_fusion.4), kind=kCustom, calls=%fused_computation.1.clone.clone.1 | custom fusion | bytes 262160 | tf_op jit(solution)/shard_map/while/body/eval_jaxpr/jit(_take)/gather | solution.py:31
  70.3 0.1 bitcast_select_fusion.5
  70.6 0.7 convert_bitcast_fusion.3
  71.3 0.4 fusion.56
  71.8 0.1 compare_and_fusion.4
  71.8 1.7 %gather_fusion = bf16[4,128,128]{2,1,0:T(8,128)(2,1)S(1)} fusion(bf16[24,128,128]{2,1,0:T(8,128)(2,1)} %bitcast.136, s32[1024]{0:T(1024)S(1)} %pad_clamp_fusion.4), kind=kCustom, calls=%fused_computation.3.clone.clone.1 | custom fusion | bytes 262160 | tf_op jit(solution)/shard_map/while/body/eval_jaxpr/jit(_take)/gather | solution.py:28
  73.6 1.7 %gather_fusion.1 = bf16[4,128,128]{2,1,0:T(8,128)(2,1)S(1)} fusion(bf16[24,128,128]{2,1,0:T(8,128)(2,1)} %bitcast.134, s32[1024]{0:T(1024)S(1)} %pad_clamp_fusion.4), kind=kCustom, calls=%fused_computation.1.clone.clone.1 | custom fusion | bytes 262160 | tf_op jit(solution)/shard_map/while/body/eval_jaxpr/jit(_take)/gather | solution.py:31
  75.3 0.1 bitcast_select_fusion.5
  75.5 0.7 convert_bitcast_fusion.3
  76.2 0.4 fusion.56
  76.7 0.1 reduce_sum.38
  76.8 0.2 multiply_reduce_fusion
  77.0 0.6 copy-done.2
  77.7 0.3 fusion.31
  78.0 19.5 %all-gather.1 = bf16[64,4,1024]{2,0,1:T(8,128)(2,1)S(1)} all-gather(bf16[64,4,128]{2,0,1:T(8,128)(2,1)S(1)} %fusion.31), channel_id=3, replica_groups=mesh['cache'=64,'rank'=8] {'rank'}, dimensions={2}, use_global_device_ids=true | all-gather | bytes 589824 | tf_op jit(solution)/shard_map/all_gather | solution.py:95
  97.5 0.3 fusion.15
  97.8 0.7 copy.46
  98.5 12.4 %all-to-all-start.1 = ((bf16[64,1,4,128]{3,2,1,0:T(4,128)(2,1)}), bf16[64,1,4,128]{3,2,1,0:T(4,128)(2,1)S(1)}, u32[]{:S(2)}, u32[]{:S(2)}) async-start(bf16[64,1,4,128]{3,2,1,0:T(4,128)(2,1)} %copy.46), calls=%async_computation.1 | async-start | bytes 131072 | tf_op jit(solution)/shard_map/all_to_all | solution.py:49
  110.9 9.9 %all-to-all-done.1 = bf16[64,1,4,128]{3,2,1,0:T(4,128)(2,1)S(1)} async-done(((bf16[64,1,4,128]{3,2,1,0:T(4,128)(2,1)}), bf16[64,1,4,128]{3,2,1,0:T(4,128)(2,1)S(1)}, u32[]{:S(2)}, u32[]{:S(2)}) %all-to-all-start.1) | async-done | bytes 65568 | tf_op jit(solution)/shard_map/all_to_all | solution.py:49
  120.8 0.7 gather_fusion.3
  121.4 0.8 bitcast_select_fusion.2
  (35 shorter events, 0.7 us)
Async XLA Ops:
  0.0 46.6 %copy-start = (bf16[1,1024,128]{2,1,0:T(8,128)(2,1)S(1)}, bf16[1,1024,128]{2,1,0:T(8,128)(2,1)}, u32[]{:S(2)}) copy-start(bf16[1,1024,128]{2,1,0:T(8,128)(2,1)} %param.21) | copy-start | bytes 786436
  0.0 0.7 copy-start.4
  5.0 24.6 %all-to-all-start = ((bf16[1,64,4,128]{3,2,0,1:T(4,128)(2,1)}), bf16[1,64,4,128]{3,2,0,1:T(4,128)(2,1)S(1)}, u32[]{:S(2)}, u32[]{:S(2)}) async-start(bf16[1,64,4,128]{3,2,0,1:T(4,128)(2,1)} %fusion.45), calls=%async_computation | async-start | bytes 131072 | tf_op jit(solution)/shard_map/all_to_all | solution.py:69
  20.5 0.7 copy-start.3
  76.7 1.0 copy-start.2
  78.0 19.5 %copy-start.1 = (bf16[1,1024,128]{2,1,0:T(8,128)(2,1)S(1)}, bf16[1,1024,128]{2,1,0:T(8,128)(2,1)}, u32[]{:S(2)}) copy-start(bf16[1,1024,128]{2,1,0:T(8,128)(2,1)} %param.23) | copy-start | bytes 786436
  98.5 22.3 %all-to-all-start.1 = ((bf16[64,1,4,128]{3,2,1,0:T(4,128)(2,1)}), bf16[64,1,4,128]{3,2,1,0:T(4,128)(2,1)S(1)}, u32[]{:S(2)}, u32[]{:S(2)}) async-start(bf16[64,1,4,128]{3,2,1,0:T(4,128)(2,1)} %copy.46), calls=%async_computation.1 | async-start | bytes 131072 | tf_op jit(solution)/shard_map/all_to_all | solution.py:49
where the time goes:
time: 123 us; the launch traced here: 122 us
  blocking collectives  35.3 us (29%)
  starting transfers between devices  27.3 us (22%)
  local copies, waits for them, and re-layouts  25.8 us (21%)
  waiting for transfers between devices  18.3 us (15%)
  other arithmetic  10.9 us (9%)
  matrix products  3.56 us (3%)
    all_gather x1, blocking collectives, on_device(): lax.all_gather(hidden, 'rank', axis=3, tiled=True)  19.5 us
    all_gather x1, blocking collectives, on_device(): whole_rows = lax.all_gather(current, 'rank', axis=3, tiled=True)  15.8 us
    all_to_all x1, starting transfers between devices, on_device(): lax.all_to_all(outgoing, 'cache', split_axis=1, concat_axis=0, tiled=True)  14.8 us
    all_to_all x1, starting transfers between devices, finish(): lax.all_to_all(result, 'cache', split_axis=0, concat_axis=1, tiled=True)  12.4 us
    gather x6, local copies, waits for them, and re-layouts, one_turn(): jnp.take(key_cache, chosen, axis=0)  10.2 us
    gather x6, local copies, waits for them, and re-layouts, one_turn(): jnp.take(value_cache, chosen, axis=0)  10.2 us
    all_to_all x1, waiting for transfers between devices, finish(): lax.all_to_all(result, 'cache', split_axis=0, concat_axis=1, tiled=True)  9.87 us
    all_to_all x1, waiting for transfers between devices, on_device(): lax.all_to_all(outgoing, 'cache', split_axis=1, concat_axis=0, tiled=True)  8.45 us
  transfers between devices with their start and end apart: 2, of which 2 were waited for; matrix products, arithmetic and copies ran while one was open for 0% of the time, Pallas kernels for 0%

commit v1 on v0

--- a/solution.py
+++ b/solution.py
@@ -90,11 +90,12 @@
         .astype(jnp.bfloat16)
     )
     rows_in = w_out[0]
+    assign_the_levels_all = lambda inputs: jnp.concatenate(
+        lax.all_to_all(jnp.stack([inputs for _ in range(lax.axis_size("rank"))]), "rank", 0, 0),
+        axis=3,
+    )
     projected = jnp.einsum(
-        "nukd,de->nuke",
-        lax.all_gather(hidden, "rank", axis=3, tiled=True),
-        rows_in,
-        preferred_element_type=jnp.float32,
+        "nukd,de->nuke", assign_the_levels_all(hidden), rows_in, preferred_element_type=jnp.float32
     )
     current = (current.astype(jnp.float32) + projected).astype(jnp.bfloat16)
     returned = finish(current)

time: 123 us -> 121 us (0.984)
  blocking collectives: 35.3 us -> 15.8 us
  waiting for transfers between devices: 18.3 us -> 31.4 us
  local copies, waits for them, and re-layouts: 25.8 us -> 27.9 us
  starting transfers between devices: 27.3 us -> 29.1 us
    all_gather x1 -> x0, blocking collectives: 19.5 us -> none  [on_device(): lax.all_gather(hidden, 'rank', axis=3, tiled=True)]
    all_to_all x0 -> x1, waiting for transfers between devices: none -> 13.1 us  [on_device(): lax.all_to_all(jnp.stack([inputs for _ in range(lax.axis_size('rank'))]),...]
    all_to_all x0 -> x1, starting transfers between devices: none -> 4.89 us  [on_device(): lax.all_to_all(jnp.stack([inputs for _ in range(lax.axis_size('rank'))]),...]
    all_to_all x1, starting transfers between devices: 12.4 us -> 9.4 us  [finish(): lax.all_to_all(result, 'cache', split_axis=0, concat_axis=1, tiled=True)]
  transfers between devices with their start and end apart: 2 -> 3, of which waited for: 2 -> 3; matrix products, arithmetic and copies ran while one was open for 0% -> 0% of each run, Pallas kernels for 0% -> 0%
where the time goes in v1:
time: 121 us; the launch traced here: 120 us
  waiting for transfers between devices  31.4 us (26%)
  starting transfers between devices  29.1 us (24%)
  local copies, waits for them, and re-layouts  27.9 us (23%)
  blocking collectives  15.8 us (13%)
  other arithmetic  10.9 us (9%)
  matrix products  3.57 us (3%)
    all_gather x1, blocking collectives, on_device(): whole_rows = lax.all_gather(current, 'rank', axis=3, tiled=True)  15.8 us
    all_to_all x1, starting transfers between devices, on_device(): lax.all_to_all(outgoing, 'cache', split_axis=1, concat_axis=0, tiled=True)  14.8 us
    all_to_all x1, waiting for transfers between devices, on_device(): lax.all_to_all(jnp.stack([inputs for _ in range(lax.axis_size('rank'))]),...  13.1 us
    gather x6, local copies, waits for them, and re-layouts, one_turn(): jnp.take(value_cache, chosen, axis=0)  10.2 us
    gather x6, local copies, waits for them, and re-layouts, one_turn(): jnp.take(key_cache, chosen, axis=0)  10.2 us
    all_to_all x1, waiting for transfers between devices, finish(): lax.all_to_all(result, 'cache', split_axis=0, concat_axis=1, tiled=True)  9.87 us
    all_to_all x1, starting transfers between devices, finish(): lax.all_to_all(result, 'cache', split_axis=0, concat_axis=1, tiled=True)  9.4 us
    all_to_all x1, waiting for transfers between devices, on_device(): lax.all_to_all(outgoing, 'cache', split_axis=1, concat_axis=0, tiled=True)  8.46 us
  transfers between devices with their start and end apart: 3, of which 3 were waited for; matrix products, arithmetic and copies ran while one was open for 0% of the time, Pallas kernels for 0%

profile of v1, /device:TPU:1, one launch (start us, length us, event | category | flops | bytes accessed | tf_op | source)
XLA Modules:
  0.0 119.9 jit_solution(5113821395280949704)
XLA Ops:
  0.0 0.7 copy-done.4
  0.7 2.0 %sort.17 = (s32[64]{0:T(128)}, s32[64]{0:T(128)S(1)}) sort(s32[64]{0:T(128)S(1)} %copy-done.4, s32[64]{0:T(128)S(1)} %iota.13), dimensions={0}, to_apply=%region_0.0 | sort | flops 384 | bytes 1024 | tf_op jit(solution)/shard_map/jit(argsort)/sort | solution.py:60
  2.8 1.5 %gather_fusion.2 = bf16[64,4,128]{2,1,0:T(4,128)(2,1)S(1)} fusion(bf16[64,4,128]{2,1,0:T(4,128)(2,1)} %bitcast.144, s32[1024]{0:T(1024)S(1)} %pad_clamp_fusion.2), kind=kCustom, calls=%fused_computation.clone | custom fusion | bytes 131328 | tf_op jit(solution)/shard_map/jit(_take)/gather | solution.py:61
  4.3 0.8 fusion.45
  5.0 14.8 %all-to-all-start = ((bf16[1,64,4,128]{3,2,0,1:T(4,128)(2,1)}), bf16[1,64,4,128]{3,2,0,1:T(4,128)(2,1)S(1)}, u32[]{:S(2)}, u32[]{:S(2)}) async-start(bf16[1,64,4,128]{3,2,0,1:T(4,128)(2,1)} %fusion.45), calls=%async_computation | async-start | bytes 131072 | tf_op jit(solution)/shard_map/all_to_all | solution.py:69
  20.5 0.6 copy-done.3
  21.2 8.5 %all-to-all-done = bf16[1,64,4,128]{3,2,0,1:T(4,128)(2,1)S(1)} async-done(((bf16[1,64,4,128]{3,2,0,1:T(4,128)(2,1)}), bf16[1,64,4,128]{3,2,0,1:T(4,128)(2,1)S(1)}, u32[]{:S(2)}, u32[]{:S(2)}) %all-to-all-start) | async-done | bytes 65568 | tf_op jit(solution)/shard_map/all_to_all | solution.py:69
  29.7 15.8 %all-gather = bf16[1,64,4,1024]{3,2,0,1:T(4,128)(2,1)S(1)} all-gather(bf16[1,64,4,128]{3,2,0,1:T(4,128)(2,1)S(1)} %all-to-all-done), channel_id=2, replica_groups=mesh['cache'=64,'rank'=8] {'rank'}, dimensions={3}, use_global_device_ids=true | all-gather | bytes 589824 | tf_op jit(solution)/shard_map/all_gather | solution.py:70
  45.5 0.3 convert_reduce_fusion
  45.8 0.5 fusion.19
  46.3 0.3 fusion.21
  46.6 0.3 fusion.40
  47.0 29.7 %while.14 = (s32[]{:T(128)}, f32[64,4,1,128]{3,0,1,2:T(8,128)S(1)}, s32[24]{0:T(128)S(1)}, bf16[24,128,1,128]{3,1,0,2:T(8,128)(2,1)}, bf16[24,128,1,128]{3,1,0,2...) while((s32[]{:T(128)}, f32[64,4,1,128]{3,0,1,2:T(8,128)S(1)}, ...), condition=%wide.region_4.7_spmd.clone, body=%wide.region_3.6_spmd.clone.sunk | while | flops 68226080 | bytes 1646929 | solution.py:45
  47.0 0.1 compare_and_fusion.4
  47.1 1.7 %gather_fusion = bf16[4,128,128]{2,1,0:T(8,128)(2,1)S(1)} fusion(bf16[24,128,128]{2,1,0:T(8,128)(2,1)} %bitcast.142, s32[1024]{0:T(1024)S(1)} %pad_clamp_fusion.4), kind=kCustom, calls=%fused_computation.3.clone.clone.1 | custom fusion | bytes 262160 | tf_op jit(solution)/shard_map/while/body/eval_jaxpr/jit(_take)/gather | solution.py:28
  48.8 1.7 %gather_fusion.1 = bf16[4,128,128]{2,1,0:T(8,128)(2,1)S(1)} fusion(bf16[24,128,128]{2,1,0:T(8,128)(2,1)} %bitcast.140, s32[1024]{0:T(1024)S(1)} %pad_clamp_fusion.4), kind=kCustom, calls=%fused_computation.1.clone.clone.1 | custom fusion | bytes 262160 | tf_op jit(solution)/shard_map/while/body/eval_jaxpr/jit(_take)/gather | solution.py:31
  50.5 0.1 bitcast_select_fusion.5
  50.8 0.7 convert_bitcast_fusion.3
  51.5 0.4 fusion.56
  51.9 0.1 compare_and_fusion.4
  52.0 1.7 %gather_fusion = bf16[4,128,128]{2,1,0:T(8,128)(2,1)S(1)} fusion(bf16[24,128,128]{2,1,0:T(8,128)(2,1)} %bitcast.142, s32[1024]{0:T(1024)S(1)} %pad_clamp_fusion.4), kind=kCustom, calls=%fused_computation.3.clone.clone.1 | custom fusion | bytes 262160 | tf_op jit(solution)/shard_map/while/body/eval_jaxpr/jit(_take)/gather | solution.py:28
  53.7 1.7 %gather_fusion.1 = bf16[4,128,128]{2,1,0:T(8,128)(2,1)S(1)} fusion(bf16[24,128,128]{2,1,0:T(8,128)(2,1)} %bitcast.140, s32[1024]{0:T(1024)S(1)} %pad_clamp_fusion.4), kind=kCustom, calls=%fused_computation.1.clone.clone.1 | custom fusion | bytes 262160 | tf_op jit(solution)/shard_map/while/body/eval_jaxpr/jit(_take)/gather | solution.py:31
  55.5 0.1 bitcast_select_fusion.5
  55.7 0.7 convert_bitcast_fusion.3
  56.4 0.4 fusion.56
  56.9 0.1 compare_and_fusion.4
  57.0 1.7 %gather_fusion = bf16[4,128,128]{2,1,0:T(8,128)(2,1)S(1)} fusion(bf16[24,128,128]{2,1,0:T(8,128)(2,1)} %bitcast.142, s32[1024]{0:T(1024)S(1)} %pad_clamp_fusion.4), kind=kCustom, calls=%fused_computation.3.clone.clone.1 | custom fusion | bytes 262160 | tf_op jit(solution)/shard_map/while/body/eval_jaxpr/jit(_take)/gather | solution.py:28
  58.7 1.7 %gather_fusion.1 = bf16[4,128,128]{2,1,0:T(8,128)(2,1)S(1)} fusion(bf16[24,128,128]{2,1,0:T(8,128)(2,1)} %bitcast.140, s32[1024]{0:T(1024)S(1)} %pad_clamp_fusion.4), kind=kCustom, calls=%fused_computation.1.clone.clone.1 | custom fusion | bytes 262160 | tf_op jit(solution)/shard_map/while/body/eval_jaxpr/jit(_take)/gather | solution.py:31
  60.4 0.1 bitcast_select_fusion.5
  60.7 0.7 convert_bitcast_fusion.3
  61.4 0.4 fusion.56
  61.9 0.1 compare_and_fusion.4
  61.9 1.7 %gather_fusion = bf16[4,128,128]{2,1,0:T(8,128)(2,1)S(1)} fusion(bf16[24,128,128]{2,1,0:T(8,128)(2,1)} %bitcast.142, s32[1024]{0:T(1024)S(1)} %pad_clamp_fusion.4), kind=kCustom, calls=%fused_computation.3.clone.clone.1 | custom fusion | bytes 262160 | tf_op jit(solution)/shard_map/while/body/eval_jaxpr/jit(_take)/gather | solution.py:28
  63.7 1.7 %gather_fusion.1 = bf16[4,128,128]{2,1,0:T(8,128)(2,1)S(1)} fusion(bf16[24,128,128]{2,1,0:T(8,128)(2,1)} %bitcast.140, s32[1024]{0:T(1024)S(1)} %pad_clamp_fusion.4), kind=kCustom, calls=%fused_computation.1.clone.clone.1 | custom fusion | bytes 262160 | tf_op jit(solution)/shard_map/while/body/eval_jaxpr/jit(_take)/gather | solution.py:31
  65.4 0.1 bitcast_select_fusion.5
  65.6 0.7 convert_bitcast_fusion.3
  66.3 0.4 fusion.56
  66.8 0.1 compare_and_fusion.4
  66.9 1.7 %gather_fusion = bf16[4,128,128]{2,1,0:T(8,128)(2,1)S(1)} fusion(bf16[24,128,128]{2,1,0:T(8,128)(2,1)} %bitcast.142, s32[1024]{0:T(1024)S(1)} %pad_clamp_fusion.4), kind=kCustom, calls=%fused_computation.3.clone.clone.1 | custom fusion | bytes 262160 | tf_op jit(solution)/shard_map/while/body/eval_jaxpr/jit(_take)/gather | solution.py:28
  68.6 1.7 %gather_fusion.1 = bf16[4,128,128]{2,1,0:T(8,128)(2,1)S(1)} fusion(bf16[24,128,128]{2,1,0:T(8,128)(2,1)} %bitcast.140, s32[1024]{0:T(1024)S(1)} %pad_clamp_fusion.4), kind=kCustom, calls=%fused_computation.1.clone.clone.1 | custom fusion | bytes 262160 | tf_op jit(solution)/shard_map/while/body/eval_jaxpr/jit(_take)/gather | solution.py:31
  70.3 0.1 bitcast_select_fusion.5
  70.6 0.7 convert_bitcast_fusion.3
  71.3 0.4 fusion.56
  71.9 1.7 %gather_fusion = bf16[4,128,128]{2,1,0:T(8,128)(2,1)S(1)} fusion(bf16[24,128,128]{2,1,0:T(8,128)(2,1)} %bitcast.142, s32[1024]{0:T(1024)S(1)} %pad_clamp_fusion.4), kind=kCustom, calls=%fused_computation.3.clone.clone.1 | custom fusion | bytes 262160 | tf_op jit(solution)/shard_map/while/body/eval_jaxpr/jit(_take)/gather | solution.py:28
  73.6 1.7 %gather_fusion.1 = bf16[4,128,128]{2,1,0:T(8,128)(2,1)S(1)} fusion(bf16[24,128,128]{2,1,0:T(8,128)(2,1)} %bitcast.140, s32[1024]{0:T(1024)S(1)} %pad_clamp_fusion.4), kind=kCustom, calls=%fused_computation.1.clone.clone.1 | custom fusion | bytes 262160 | tf_op jit(solution)/shard_map/while/body/eval_jaxpr/jit(_take)/gather | solution.py:31
  75.3 0.1 bitcast_select_fusion.5
  75.5 0.7 convert_bitcast_fusion.3
  76.3 0.4 fusion.56
  76.7 0.1 reduce_sum.38
  76.9 0.2 multiply_reduce_fusion
  77.0 0.6 copy-done.2
  77.7 0.3 fusion.31
  78.0 0.9 stack.5
  78.9 4.9 %all-to-all-start.1 = ((bf16[8,64,1,4,128]{4,1,3,2,0:T(8,128)(2,1)}), bf16[8,64,1,4,128]{4,1,3,2,0:T(8,128)(2,1)S(1)}, u32[]{:S(2)}, u32[]{:S(2)}) async-start(bf16[8,64,1,4,128]{4,1,3,2,0:T(8,128)(2,1)} %stack.5), calls=%async_computation.1 | async-start | bytes 1048576 | tf_op jit(solution)/shard_map/all_to_all | solution.py:94
  83.8 13.1 %all-to-all-done.1 = bf16[8,64,1,4,128]{4,1,3,2,0:T(8,128)(2,1)S(1)} async-done(((bf16[8,64,1,4,128]{4,1,3,2,0:T(8,128)(2,1)}), bf16[8,64,1,4,128]{4,1,3,2,0:T(8,128)(2,1)S(1)}, u32[]{:S(2)}, u32[]{:S(2)}) %all-to-all-start.1) | async-done | bytes 524320 | tf_op jit(solution)/shard_map/all_to_all | solution.py:94
  96.9 0.3 copy.49
  97.3 0.2 reshape.222
  97.5 0.7 copy-done.1
  98.2 0.3 fusion.15
  98.5 0.7 copy.50
  99.2 9.4 %all-to-all-start.2 = ((bf16[64,1,4,128]{3,2,1,0:T(4,128)(2,1)}), bf16[64,1,4,128]{3,2,1,0:T(4,128)(2,1)S(1)}, u32[]{:S(2)}, u32[]{:S(2)}) async-start(bf16[64,1,4,128]{3,2,1,0:T(4,128)(2,1)} %copy.50), calls=%async_computation.2 | async-start | bytes 131072 | tf_op jit(solution)/shard_map/all_to_all | solution.py:49
  108.6 9.9 %all-to-all-done.2 = bf16[64,1,4,128]{3,2,1,0:T(4,128)(2,1)S(1)} async-done(((bf16[64,1,4,128]{3,2,1,0:T(4,128)(2,1)}), bf16[64,1,4,128]{3,2,1,0:T(4,128)(2,1)S(1)}, u32[]{:S(2)}, u32[]{:S(2)}) %all-to-all-start.2) | async-done | bytes 65568 | tf_op jit(solution)/shard_map/all_to_all | solution.py:49
  118.5 0.7 gather_fusion.3
  119.1 0.8 bitcast_select_fusion.2
  (39 shorter events, 1.1 us)
Async XLA Ops:
  0.0 46.6 %copy-start = (bf16[1,1024,128]{2,1,0:T(8,128)(2,1)S(1)}, bf16[1,1024,128]{2,1,0:T(8,128)(2,1)}, u32[]{:S(2)}) copy-start(bf16[1,1024,128]{2,1,0:T(8,128)(2,1)} %param.21) | copy-start | bytes 786436
  0.0 0.7 copy-start.4
  5.0 24.6 %all-to-all-start = ((bf16[1,64,4,128]{3,2,0,1:T(4,128)(2,1)}), bf16[1,64,4,128]{3,2,0,1:T(4,128)(2,1)S(1)}, u32[]{:S(2)}, u32[]{:S(2)}) async-start(bf16[1,64,4,128]{3,2,0,1:T(4,128)(2,1)} %fusion.45), calls=%async_computation | async-start | bytes 131072 | tf_op jit(solution)/shard_map/all_to_all | solution.py:69
  20.5 0.7 copy-start.3
  76.7 1.0 copy-start.2
  78.9 18.0 %all-to-all-start.1 = ((bf16[8,64,1,4,128]{4,1,3,2,0:T(8,128)(2,1)}), bf16[8,64,1,4,128]{4,1,3,2,0:T(8,128)(2,1)S(1)}, u32[]{:S(2)}, u32[]{:S(2)}) async-start(bf16[8,64,1,4,128]{4,1,3,2,0:T(8,128)(2,1)} %stack.5), calls=%async_computation.1 | async-start | bytes 1048576 | tf_op jit(solution)/shard_map/all_to_all | solution.py:94
  97.2 1.0 copy-start.1
  99.2 19.3 %all-to-all-start.2 = ((bf16[64,1,4,128]{3,2,1,0:T(4,128)(2,1)}), bf16[64,1,4,128]{3,2,1,0:T(4,128)(2,1)S(1)}, u32[]{:S(2)}, u32[]{:S(2)}) async-start(bf16[64,1,4,128]{3,2,1,0:T(4,128)(2,1)} %copy.50), calls=%async_computation.2 | async-start | bytes 131072 | tf_op jit(solution)/shard_map/all_to_all | solution.py:49
